TPU v7x, 512 devices: a whole 4x4x16 slice. The times are simulated.
512 devices in a mesh: row: 32 (over z, x_lo), rep: 16 (over x_hi, y, core).
Axes of the slice: x: 4 (x_hi: 2, x_lo: 2; x = x_hi * 2 + x_lo), y: 4, z: 16, core: 2. Of those that a mesh axis runs over, the one named last changes fastest.
Arguments:
- features: bfloat16 [131072, 256], P(('row', 'rep')), may hold values from -6 to 6
- dense_blocks: bfloat16 [131072, 2, 4096], P('row', None, 'rep'), may hold values from -0.0625 to 0.0625
- thick_neighbour_labels: int32 [32, 2], P('row'), may hold values from 0 to 31, as said below
- tile_source: int32 [32, 16, 64], P('row', 'rep'), may hold values from 0 to 63, as said below
- tile_dest: int32 [32, 16, 64], P('row', 'rep'), may hold values from 0 to 31
- entry_rows: int32 [32, 16, 64, 512], P('row', 'rep'), may hold values from 0 to 127, as said below
- entry_cols: int32 [32, 16, 64, 512], P('row', 'rep'), may hold values from 0 to 127
- edge_strength_list: bfloat16 [32, 16, 64, 512], P('row', 'rep'), may hold values from -0.75 to 0.75
- entry_count: int32 [32, 16, 64], P('row', 'rep'), may hold values from 1 to 512
- weight: bfloat16 [256, 256], replicated, may hold values from -0.375 to 0.375
- out_bias: float32 [256], replicated, may hold values from -3 to 3
Outputs:
- activated: bfloat16 [131072, 256], P(('row', 'rep'))
Inputs may be any that keep to these rules, and one draw needn't show every extreme that they name: `thick_neighbour_labels`: each row block's dense source blocks are distinct and lie within cyclic distance 3 of its own block id. Within one device's list, entries with the same source row block (tile_source // 2) name the same tile. The (entry_rows, entry_cols) pairs of one sparse tile's entries are distinct.
All inputs are finite; a program needn't handle non-finite values.
Results may differ from a plain program's by a relative error of at most 0.0047.
Values may be sent and summed in bfloat16 or wider, within the bound.
A program may use at most 64 MiB of HBM per device.

v0:
```python
import jax
import jax.numpy as jnp
from jax import lax
from jax.sharding import PartitionSpec as P

FEAT = 256
TILE = 128
TILES_DEV = 2


def sparse_terms(
    src_tiles, tile_dest, entry_rows, entry_cols, edge_strength_list, entry_count, dest_tiles
):
    entry_index = lax.broadcasted_iota(jnp.int32, entry_rows.shape, 1)
    active = entry_index < entry_count[:, None]
    weights_live = jnp.where(active, edge_strength_list.astype(jnp.float32), 0.0)
    positions = lax.broadcasted_iota(jnp.int32, (1, 1, TILE), 2)
    row_onehot = (entry_rows[:, :, None] == positions).astype(jnp.bfloat16)
    col_weighted = jnp.where(
        entry_cols[:, :, None] == positions, weights_live[:, :, None], 0.0
    ).astype(jnp.bfloat16)
    tile_mats = jnp.einsum(
        "snr,snc->src", row_onehot, col_weighted, preferred_element_type=jnp.float32
    ).astype(jnp.bfloat16)
    summand_piece = jnp.einsum(
        "src,scf->srf", tile_mats, src_tiles, preferred_element_type=jnp.float32
    )
    target_onehot_mask = (
        tile_dest[None, :] == lax.broadcasted_iota(jnp.int32, (dest_tiles, 1), 0)
    ).astype(jnp.float32)
    placed_entries = jnp.einsum(
        "ou,uwd->owd", target_onehot_mask, summand_piece, precision=lax.Precision.HIGHEST
    )
    return placed_entries.reshape(dest_tiles * TILE, summand_piece.shape[2])


def shards(
    features,
    dense_blocks,
    thick_neighbour_labels,
    tile_source,
    tile_dest,
    entry_rows,
    entry_cols,
    edge_strength_list,
    entry_count,
    weight,
    out_bias,
):
    row_count = lax.axis_size("row")
    own_rows = features.shape[0]
    block_rows = dense_blocks.shape[0]
    block_ids = thick_neighbour_labels[0]
    listed = tile_source[0, 0]
    gathered = lax.all_gather(features, "row", axis=0, tiled=True)
    panel_stack = gathered.reshape(row_count, own_rows, FEAT)
    dense_panels = panel_stack[block_ids]
    src_tiles = gathered.reshape(row_count * TILES_DEV, TILE, FEAT)[listed]
    sparse_part = sparse_terms(
        src_tiles,
        tile_dest[0, 0],
        entry_rows[0, 0],
        entry_cols[0, 0],
        edge_strength_list[0, 0],
        entry_count[0, 0],
        block_rows // TILE,
    )
    dense_part = jnp.einsum(
        "nsc,scf->nf", dense_blocks, dense_panels, preferred_element_type=jnp.float32
    )
    summed = lax.psum_scatter(dense_part + sparse_part, "rep", scatter_dimension=0, tiled=True)
    hidden = summed.astype(jnp.bfloat16)
    projected = jnp.dot(hidden, weight, preferred_element_type=jnp.float32) + out_bias
    return jnp.maximum(projected, 0.0).astype(jnp.bfloat16)


def solution(mesh):
    return jax.shard_map(
        shards,
        mesh=mesh,
        in_specs=(
            P(("row", "rep"), None),
            P("row", None, "rep"),
            P("row", None),
            P("row", "rep", None),
            P("row", "rep", None),
            P("row", "rep", None, None),
            P("row", "rep", None, None),
            P("row", "rep", None, None),
            P("row", "rep", None),
            P(),
            P(),
        ),
        out_specs=P(("row", "rep"), None),
        check_vma=False,
    )
```

profile of v0, /device:TPU:32, one launch (start us, length us, event | category | flops | bytes accessed | tf_op | source)
XLA Modules:
  0.0 315.6 jit_solution(13413633316712423619)
XLA Ops:
  6.5 0.0 copy-start
  6.5 0.0 all-gather.2.cloned.1.call-start
  6.5 0.7 all-gather.2.cloned.1.call-update
  7.3 0.0 reduce-scatter.2.cloned.1.call-start
  7.3 0.7 fusion.18
  8.0 0.7 fusion.17
  8.6 0.9 convert_select_fusion
  9.6 142.9 %all-gather.2.cloned.1.call-done = bf16[8192,256]{1,0:T(8,128)(2,1)} async-done(((bf16[256,256]{1,0:T(8,128)(2,1)}), bf16[8192,256]{1,0:T(8,128)(2,1)}) %all-gather.2.cloned.1.call-update) | async-done | bytes 4194320 | tf_op jit(solution)/shard_map/all_gather | solution.py:55
  152.5 0.0 copy-start.3
  152.5 0.0 copy-start.4
  152.5 5.0 %gather_fusion.1 = bf16[64,128,256]{2,1,0:T(8,128)(2,1)} fusion(bf16[64,128,256]{2,1,0:T(8,128)(2,1)} %bitcast.32, s32[1024]{0:T(1024)S(1)} %pad_clamp_fusion), kind=kCustom, calls=%fused_computation.1 | custom fusion | bytes 8388864 | tf_op jit(solution)/shard_map/gather | solution.py:58
  157.5 0.0 copy-done.3
  157.5 0.0 copy-done.4
  157.5 22.5 %fusion.9 = f32[64,128,256]{2,1,0:T(8,128)} fusion(bf16[64,128,256]{2,1,0:T(8,128)(2,1)} %gather_fusion.1, bf16[64,512]{1,0:T(8,128)(2,1)S(1)} %convert_select_fusion, s32[64,512]{1,0:T(8,128)S(1)} %bitcast.36, s32[64,512]{1,0:T(8,128)S(1)} %bitcast.37), kind=kOutput, calls=%fused_computation.15 | convolution fusion | flops 1624244224 | bytes 12910592 | tf_op jit(solution)/shard_map/src,scf->srf/dot_general | solution.py:25
  180.0 0.0 copy-done.2
  180.0 11.3 %fusion.1 = f32[32,128,256]{2,0,1:T(8,128)S(1)} fusion(f32[64,128,256]{2,1,0:T(8,128)} %fusion.9, s32[64]{0:T(128)S(1)} %bitcast.35), kind=kOutput, calls=%fused_computation.6 | convolution fusion | flops 805308416 | bytes 12583168 | tf_op jit(solution)/shard_map/ou,uwd->owd/dot_general | solution.py:31
  191.3 4.4 %copy.12 = f32[32,128,256]{2,1,0:T(8,128)} copy(f32[32,128,256]{2,0,1:T(8,128)S(1)} %fusion.1) | data formatting | bytes 8388608 | tf_op jit(solution)/shard_map/ou,uwd->owd/dot_general | solution.py:31
  195.7 2.7 gather_fusion
  198.4 6.7 %fusion.7 = f32[4096,256]{1,0:T(8,128)} fusion(f32[4096,256]{1,0:T(8,128)} %bitcast.31, bf16[2,256,256]{2,1,0:T(8,128)(2,1)S(1)} %gather_fusion, bf16[4096,2,256]{2,1,0:T(2,128)(2,1)} %param.12), kind=kOutput, calls=%fused_computation.13 | convolution fusion | flops 1074790400 | bytes 12845056 | tf_op jit(solution)/shard_map/nsc,scf->nf/dot_general | solution.py:68
  205.1 0.0 reduce-scatter.2.cloned.1.call-update
  205.1 101.8 %reduce-scatter.2.cloned.1.call-done = f32[256,256]{1,0:T(8,128)} async-done(((f32[4096,256]{1,0:T(8,128)}), f32[256,256]{1,0:T(8,128)}) %reduce-scatter.2.cloned.1.call-update) | async-done | bytes 262160 | tf_op jit(solution)/shard_map/reduce_scatter | solution.py:71
  307.0 0.0 copy-done
  307.0 0.0 copy-done.1
  307.0 1.8 fusion.12
  (4 shorter events, 0.0 us)
Async XLA Ops:
  6.5 300.4 %copy-start = (bf16[256,256]{1,0:T(8,128)(2,1)S(1)}, bf16[256,256]{1,0:T(8,128)(2,1)}, u32[]{:S(2)}) copy-start(bf16[256,256]{1,0:T(8,128)(2,1)} %param.20) | copy-start | bytes 393220
  6.5 146.0 %all-gather.2.cloned.1.call-start = ((), (), s32[]{:S(2)}) async-start(), calls=%async_computation.1 | async-start | bytes 4325376 | tf_op jit(solution)/shard_map/all_gather | solution.py:55
  7.3 299.7 %reduce-scatter.2.cloned.1.call-start = ((), (), s32[]{:S(2)}) async-start(), calls=%async_computation.2 | async-start | bytes 4456448 | tf_op jit(solution)/shard_map/reduce_scatter | solution.py:71
  152.5 5.0 %copy-start.3 = (s32[1,1,64,512]{3,2,1,0:T(8,128)S(1)}, s32[1,1,64,512]{3,2,1,0:T(8,128)}, u32[]{:S(2)}) copy-start(s32[1,1,64,512]{3,2,1,0:T(8,128)} %param.17) | copy-start | bytes 393220
  152.5 5.0 %copy-start.4 = (s32[1,1,64,512]{3,2,1,0:T(8,128)S(1)}, s32[1,1,64,512]{3,2,1,0:T(8,128)}, u32[]{:S(2)}) copy-start(s32[1,1,64,512]{3,2,1,0:T(8,128)} %param.16) | copy-start | bytes 393220
  157.5 22.5 %copy-start.2 = (s32[1,1,64]{2,1,0:T(1,128)S(1)}, s32[1,1,64]{2,1,0:T(1,128)}, u32[]{:S(2)}) copy-start(s32[1,1,64]{2,1,0:T(1,128)} %param.15) | copy-start | bytes 772
  205.1 101.8 %copy-start.1 = (f32[256]{0:T(256)S(1)}, f32[256]{0:T(256)}, u32[]{:S(2)}) copy-start(f32[256]{0:T(256)} %param.21) | copy-start | bytes 3076
Sparse Core Ops, SparseCore 0:
  9.4 143.0 all-gather.1
  205.3 101.6 reduce-scatter.1
where the time goes:
time: 316 us
  waiting for transfers between devices  245 us (78%)
  matrix products  42.3 us (13%)
  between operations  13.4 us (4%)
  local copies, waits for them, and re-layouts  12.1 us (4%)
    all_gather x1, waiting for transfers between devices, shards(): gathered = lax.all_gather(features, 'row', axis=0, tiled=True)  143 us
    reduce_scatter x1, waiting for transfers between devices, shards(): lax.psum_scatter(dense_part + sparse_part, 'rep', scatter_dimension=0, ti...  102 us
    dot_general x1, matrix products, sparse_terms(): jnp.einsum('src,scf->srf', tile_mats, src_tiles, preferred_element_type=j...  22.5 us
    dot_general x1, matrix products, sparse_terms(): jnp.einsum('ou,uwd->owd', target_onehot_mask, summand_piece, precision=la...  11.3 us
    dot_general x1, matrix products, shards(): jnp.einsum('nsc,scf->nf', dense_blocks, dense_panels, preferred_element_t...  6.71 us
  transfers between devices with their start and end apart: 2, of which 2 were waited for; matrix products, arithmetic and copies ran while one was open for 1% of the time, Pallas kernels for 0%

commit v1 on v0

--- a/solution.py
+++ b/solution.py
@@ -52,7 +52,9 @@
     block_rows = dense_blocks.shape[0]
     block_ids = thick_neighbour_labels[0]
     listed = tile_source[0, 0]
-    gathered = lax.all_gather(features, "row", axis=0, tiled=True)
+    gathered = jnp.concatenate(
+        lax.all_to_all(jnp.stack([features] * lax.axis_size("row")), "row", 0, 0), axis=0
+    )
     panel_stack = gathered.reshape(row_count, own_rows, FEAT)
     dense_panels = panel_stack[block_ids]
     src_tiles = gathered.reshape(row_count * TILES_DEV, TILE, FEAT)[listed]

time: 316 us -> 374 us (1.18)
  waiting for transfers between devices: 245 us -> 285 us
  starting transfers between devices: 0.04 us -> 16.5 us
    all_to_all x0 -> x1, waiting for transfers between devices: none -> 187 us  [shards(): lax.all_to_all(jnp.stack([features] * lax.axis_size('row')), 'row', 0, 0)]
    all_gather x1 -> x0, waiting for transfers between devices: 143 us -> none  [shards(): gathered = lax.all_gather(features, 'row', axis=0, tiled=True)]
    all_to_all x0 -> x1, starting transfers between devices: none -> 16.5 us  [shards(): lax.all_to_all(jnp.stack([features] * lax.axis_size('row')), 'row', 0, 0)]
    reduce_scatter x1, waiting for transfers between devices: 102 us -> 98 us  [shards(): lax.psum_scatter(dense_part + sparse_part, 'rep', scatter_dimension=0, ti...]
  transfers between devices with their start and end apart: 2 -> 2, of which waited for: 2 -> 2; matrix products, arithmetic and copies ran while one was open for 1% -> 0% of each run, Pallas kernels for 0% -> 0%
where the time goes in v1:
time: 374 us; the launch traced here: 373 us
  waiting for transfers between devices  285 us (76%)
  matrix products  42.3 us (11%)
  starting transfers between devices  16.5 us (4%)
  local copies, waits for them, and re-layouts  15.5 us (4%)
  between operations  13.5 us (4%)
    all_to_all x1, waiting for transfers between devices, shards(): lax.all_to_all(jnp.stack([features] * lax.axis_size('row')), 'row', 0, 0)  187 us
    reduce_scatter x1, waiting for transfers between devices, shards(): lax.psum_scatter(dense_part + sparse_part, 'rep', scatter_dimension=0, ti...  98 us
    dot_general x1, matrix products, sparse_terms(): jnp.einsum('src,scf->srf', tile_mats, src_tiles, preferred_element_type=j...  22.5 us
    all_to_all x1, starting transfers between devices, shards(): lax.all_to_all(jnp.stack([features] * lax.axis_size('row')), 'row', 0, 0)  16.5 us
    dot_general x1, matrix products, sparse_terms(): jnp.einsum('ou,uwd->owd', target_onehot_mask, summand_piece, precision=la...  11.3 us
  transfers between devices with their start and end apart: 2, of which 2 were waited for; matrix products, arithmetic and copies ran while one was open for 0% of the time, Pallas kernels for 0%

profile of v1, /device:TPU:32, one launch (start us, length us, event | category | flops | bytes accessed | tf_op | source)
XLA Modules:
  0.0 373.3 jit_solution(7078012889984156031)
XLA Ops:
  6.5 0.0 copy-start
  6.5 3.4 stack.2
  9.9 16.5 %all-to-all-start = ((bf16[32,256,256]{2,1,0:T(8,128)(2,1)}), bf16[32,256,256]{2,1,0:T(8,128)(2,1)}, u32[]{:S(2)}, u32[]{:S(2)}) async-start(bf16[32,256,256]{2,1,0:T(8,128)(2,1)} %stack.2), calls=%async_computation | async-start | bytes 8388608 | tf_op jit(solution)/shard_map/all_to_all | solution.py:56
  26.4 0.0 reduce-scatter.2.cloned.1.call-start
  26.5 0.0 copy-done.7
  26.5 0.0 copy-done.8
  26.5 0.0 copy-done.1
  26.5 0.0 copy-done.3
  26.5 0.1 convert_select_fusion
  26.6 187.4 %all-to-all-done = bf16[32,256,256]{2,1,0:T(8,128)(2,1)} async-done(((bf16[32,256,256]{2,1,0:T(8,128)(2,1)}), bf16[32,256,256]{2,1,0:T(8,128)(2,1)}, u32[]{:S(2)}, u32[]{:S(2)}) %all-to-all-start) | async-done | bytes 4194336 | tf_op jit(solution)/shard_map/all_to_all | solution.py:56
  214.0 5.0 %gather_fusion.1 = bf16[64,128,256]{2,1,0:T(8,128)(2,1)} fusion(bf16[64,128,256]{2,1,0:T(8,128)(2,1)} %bitcast.10, s32[1024]{0:T(1024)S(1)} %pad_clamp_fusion), kind=kCustom, calls=%fused_computation.1 | custom fusion | bytes 8388864 | tf_op jit(solution)/shard_map/gather | solution.py:60
  219.0 0.0 copy-done.5
  219.0 0.0 copy-done.6
  219.0 22.5 %fusion.9 = f32[64,128,256]{2,1,0:T(8,128)} fusion(bf16[64,128,256]{2,1,0:T(8,128)(2,1)} %gather_fusion.1, bf16[64,512]{1,0:T(8,128)(2,1)S(1)} %convert_select_fusion, s32[64,512]{1,0:T(8,128)S(1)} %bitcast.33, s32[64,512]{1,0:T(8,128)S(1)} %bitcast.34), kind=kOutput, calls=%fused_computation.15 | convolution fusion | flops 1624244224 | bytes 12910592 | tf_op jit(solution)/shard_map/src,scf->srf/dot_general | solution.py:25
  241.5 0.0 copy-done.4
  241.5 11.3 %fusion.1 = f32[32,128,256]{2,0,1:T(8,128)S(1)} fusion(f32[64,128,256]{2,1,0:T(8,128)} %fusion.9, s32[64]{0:T(128)S(1)} %bitcast.32), kind=kOutput, calls=%fused_computation.6 | convolution fusion | flops 805308416 | bytes 12583168 | tf_op jit(solution)/shard_map/ou,uwd->owd/dot_general | solution.py:31
  252.8 4.4 %copy.12 = f32[32,128,256]{2,1,0:T(8,128)} copy(f32[32,128,256]{2,0,1:T(8,128)S(1)} %fusion.1) | data formatting | bytes 8388608 | tf_op jit(solution)/shard_map/ou,uwd->owd/dot_general | solution.py:31
  257.2 2.7 gather_fusion
  259.9 6.7 %fusion.7 = f32[4096,256]{1,0:T(8,128)} fusion(f32[4096,256]{1,0:T(8,128)} %bitcast.30, bf16[2,256,256]{2,1,0:T(8,128)(2,1)S(1)} %gather_fusion, bf16[4096,2,256]{2,1,0:T(2,128)(2,1)} %param.12), kind=kOutput, calls=%fused_computation.13 | convolution fusion | flops 1074790400 | bytes 12845056 | tf_op jit(solution)/shard_map/nsc,scf->nf/dot_general | solution.py:70
  266.6 0.0 reduce-scatter.2.cloned.1.call-update
  266.7 98.0 %reduce-scatter.2.cloned.1.call-done = f32[256,256]{1,0:T(8,128)} async-done(((f32[4096,256]{1,0:T(8,128)}), f32[256,256]{1,0:T(8,128)}) %reduce-scatter.2.cloned.1.call-update) | async-done | bytes 262160 | tf_op jit(solution)/shard_map/reduce_scatter | solution.py:73
  364.7 0.0 copy-done
  364.7 0.0 copy-done.2
  364.7 1.8 fusion.12
  (12 shorter events, 0.0 us)
Async XLA Ops:
  6.5 358.1 %copy-start = (bf16[256,256]{1,0:T(8,128)(2,1)S(1)}, bf16[256,256]{1,0:T(8,128)(2,1)}, u32[]{:S(2)}) copy-start(bf16[256,256]{1,0:T(8,128)(2,1)} %param.20) | copy-start | bytes 393220
  9.9 16.6 %copy-start.7 = (s32[1,1,64]{2,1,0:T(1,128)S(1)}, s32[1,1,64]{2,1,0:T(1,128)}, u32[]{:S(2)}) copy-start(s32[1,1,64]{2,1,0:T(1,128)} %param.14) | copy-start | bytes 772
  9.9 16.6 %copy-start.8 = (s32[1,2]{1,0:T(1,128)S(1)}, s32[1,2]{1,0:T(1,128)}, u32[]{:S(2)}) copy-start(s32[1,2]{1,0:T(1,128)} %param.13) | copy-start | bytes 28
  9.9 16.6 %copy-start.1 = (bf16[1,1,64,512]{3,2,1,0:T(8,128)(2,1)S(1)}, bf16[1,1,64,512]{3,2,1,0:T(8,128)(2,1)}, u32[]{:S(2)}) copy-start(bf16[1,1,64,512]{3,2,1,0:T(8,128)(2,1)} %param.18) | copy-start | bytes 196612
  9.9 16.6 %copy-start.3 = (s32[1,1,64]{2,1,0:T(1,128)S(1)}, s32[1,1,64]{2,1,0:T(1,128)}, u32[]{:S(2)}) copy-start(s32[1,1,64]{2,1,0:T(1,128)} %param.19) | copy-start | bytes 772
  9.9 204.1 %all-to-all-start = ((bf16[32,256,256]{2,1,0:T(8,128)(2,1)}), bf16[32,256,256]{2,1,0:T(8,128)(2,1)}, u32[]{:S(2)}, u32[]{:S(2)}) async-start(bf16[32,256,256]{2,1,0:T(8,128)(2,1)} %stack.2), calls=%async_computation | async-start | bytes 8388608 | tf_op jit(solution)/shard_map/all_to_all | solution.py:56
  26.4 338.3 %reduce-scatter.2.cloned.1.call-start = ((), (), s32[]{:S(2)}) async-start(), calls=%async_computation.2 | async-start | bytes 4456448 | tf_op jit(solution)/shard_map/reduce_scatter | solution.py:73
  214.0 5.0 %copy-start.5 = (s32[1,1,64,512]{3,2,1,0:T(8,128)S(1)}, s32[1,1,64,512]{3,2,1,0:T(8,128)}, u32[]{:S(2)}) copy-start(s32[1,1,64,512]{3,2,1,0:T(8,128)} %param.17) | copy-start | bytes 393220
  214.0 5.0 %copy-start.6 = (s32[1,1,64,512]{3,2,1,0:T(8,128)S(1)}, s32[1,1,64,512]{3,2,1,0:T(8,128)}, u32[]{:S(2)}) copy-start(s32[1,1,64,512]{3,2,1,0:T(8,128)} %param.16) | copy-start | bytes 393220
  219.0 22.5 %copy-start.4 = (s32[1,1,64]{2,1,0:T(1,128)S(1)}, s32[1,1,64]{2,1,0:T(1,128)}, u32[]{:S(2)}) copy-start(s32[1,1,64]{2,1,0:T(1,128)} %param.15) | copy-start | bytes 772
  266.6 98.1 %copy-start.2 = (f32[256]{0:T(256)S(1)}, f32[256]{0:T(256)}, u32[]{:S(2)}) copy-start(f32[256]{0:T(256)} %param.21) | copy-start | bytes 3076
Sparse Core Ops, SparseCore 0:
  266.8 97.8 reduce-scatter.1
